TPU v7x, 256 devices: a whole 4x4x8 slice. The times are simulated.
256 devices in a mesh: walker: 64 (over x_hi, y, z), freq: 4 (over x_lo, core).
Axes of the slice: x: 4 (x_hi: 2, x_lo: 2; x = x_hi * 2 + x_lo), y: 4, z: 8, core: 2. Of those that a mesh axis runs over, the one named last changes fastest.
Arguments:
- green_up_blocks: bfloat16 [64, 1, 4, 4288], P('walker', None, 'freq'), may hold values from -6 to 6
- green_down_blocks: bfloat16 [64, 1, 4, 4288], P('walker', None, 'freq'), may hold values from -6 to 6
- nu_index: int32 [4], P('freq'), may hold values from 0 to 3, each once
- q_index: int32 [4], P('freq'), may hold values from 0 to 63
- source: float32 [4, 4096], P('freq', 'walker'), may hold values from -6 to 6
Outputs:
- g4: float32 [4, 4096, 4096], P('freq', 'walker')
- response: float32 [4, 4096], P('freq', 'walker')
All inputs are finite; a program needn't handle non-finite values.
Results may differ from a plain program's by a relative error of at most 0.004.
Values may be sent and summed in bfloat16 or wider, within the bound.
No kernel may reach another device: no remote copies, remote signals or barrier semaphores. Data moves between devices by JAX's collectives and lax.ppermute only.
A program may use at most 64 MiB of HBM per device.

v0:
```python
import math

import jax
import jax.numpy as jnp
from jax import lax
from jax.sharding import PartitionSpec as P

SIDE = 8
CLUSTER_MOMENTUM = 64
W = 64
NU = 4
ITERS = 2


def cluster_sum(sites, shift):
    return (sites // SIDE + shift // SIDE) % SIDE * SIDE + (sites % SIDE + shift % SIDE) % SIDE


def products(block, sites, shift, offset):
    moved = cluster_sum(sites, shift)
    base = jnp.take(block, sites, axis=1)[:, :, :W].astype(jnp.float32)
    other = lax.dynamic_slice_in_dim(jnp.take(block, moved, axis=1), offset, W, 2).astype(
        jnp.float32
    )
    return (base * other).astype(jnp.bfloat16).reshape(block.shape[0], sites.shape[0] * W)


def stacked(block, sites, nu_index, q_index):
    return jnp.stack([products(block, sites, q_index[0], nu_index[0])])


def accumulate(left, right):
    return jnp.einsum("nrk,nrc->nkc", left, right, preferred_element_type=jnp.float32)


def shards(green_up_blocks, green_down_blocks, nu_index, q_index, source):
    up_all, down_all = (
        lax.all_gather(green_up_blocks, "freq", axis=2, tiled=True),
        lax.all_gather(green_down_blocks, "freq", axis=2, tiled=True),
    )
    extent = W + NU - 1
    rows_one = up_all.shape[1] * up_all.shape[2]
    walkers = lax.axis_size("walker")
    per_dev = CLUSTER_MOMENTUM // walkers
    owned = lax.axis_index("walker") * per_dev + jnp.arange(per_dev, dtype=jnp.int32)
    every = jnp.arange(CLUSTER_MOMENTUM, dtype=jnp.int32)

    def blocks(piece):
        return piece.reshape(-1, CLUSTER_MOMENTUM, extent)

    left = stacked(
        blocks(lax.all_gather(up_all, "walker", axis=0, tiled=True)), owned, nu_index, q_index
    )
    right = stacked(
        blocks(lax.all_gather(down_all, "walker", axis=0, tiled=True)), every, nu_index, q_index
    )
    summed = accumulate(left, right)
    kernel = summed * (1.0 / math.sqrt(walkers * rows_one))
    scale = 1.0 / (2.0 * math.sqrt(CLUSTER_MOMENTUM * W))
    start_vec = source.T
    current = start_vec
    for step in range(ITERS):

        def term(begin, sample_count, current=current):
            return jnp.einsum("kn,nkc->cn", current, kernel, precision=lax.Precision.HIGHEST)

        current = start_vec + scale * lax.psum_scatter(
            term(jnp.int32(0), lax.axis_size("walker") * (per_dev * W)),
            "walker",
            scatter_dimension=0,
            tiled=True,
        )
    return (kernel, current.T)


def solution(mesh):
    in_specs = (
        P("walker", None, "freq", None),
        P("walker", None, "freq", None),
        P("freq"),
        P("freq"),
        P("freq", "walker"),
    )
    out_specs = (P("freq", "walker", None), P("freq", "walker"))
    return jax.shard_map(shards, mesh=mesh, in_specs=in_specs, out_specs=out_specs, check_vma=False)
```

profile of v0, /device:TPU:6, one launch (start us, length us, event | category | flops | bytes accessed | tf_op | source)
XLA Modules:
  0.0 1024.6 jit_solution(13348956791322953057)
XLA Ops:
  7.2 0.0 all-gather.3.cloned.1.call-start
  7.2 5.5 all_gather.12
  12.7 0.6 copy.18
  13.3 0.0 all-gather.3.cloned.1.call-update
  13.3 0.0 all-gather.5.cloned.1.call-start
  13.4 5.5 all_gather.14
  18.8 0.6 copy.22
  19.5 0.0 all-gather.5.cloned.1.call-update
  19.5 0.0 reduce-scatter.7.cloned.1.call-start
  21.0 112.8 %all-gather.3.cloned.1.call-done = bf16[64,1,4,4288]{3,2,1,0:T(4,128)(2,1)} async-done(((bf16[1,1,4,4288]{3,2,1,0:T(4,128)(2,1)}), bf16[64,1,4,4288]{3,2,1,0:T(4,128)(2,1)}) %all-gather.3.cloned.1.call-update) | async-done | bytes 2195472 | tf_op jit(solution)/shard_map/all_gather | solution.py:52
  133.8 15.4 %reshape.59 = bf16[256,64,67]{2,1,0:T(8,128)(2,1)} reshape(bf16[64,1,4,4288]{3,2,1,0:T(4,128)(2,1)} %all-gather.3.cloned.1.call-done) | data formatting | bytes 4390912 | tf_op jit(solution)/shard_map/reshape | solution.py:49
  149.2 1.5 constant_dynamic-slice_fusion.1
  150.7 0.2 constant_dynamic-slice_fusion.2
  150.9 0.1 copy.32
  151.0 0.1 copy.31
  151.1 102.5 %all-gather.5.cloned.1.call-done = bf16[64,1,4,4288]{3,2,1,0:T(4,128)(2,1)} async-done(((bf16[1,1,4,4288]{3,2,1,0:T(4,128)(2,1)}), bf16[64,1,4,4288]{3,2,1,0:T(4,128)(2,1)}) %all-gather.5.cloned.1.call-update) | async-done | bytes 2195472 | tf_op jit(solution)/shard_map/all_gather | solution.py:55
  253.7 15.4 %reshape.61 = bf16[256,64,67]{2,1,0:T(8,128)(2,1)} reshape(bf16[64,1,4,4288]{3,2,1,0:T(4,128)(2,1)} %all-gather.5.cloned.1.call-done) | data formatting | bytes 4390912 | tf_op jit(solution)/shard_map/reshape | solution.py:49
  269.1 6.7 copy.23
  275.8 2.1 gather_fusion.1
  277.9 2.1 gather_fusion
  280.0 2.9 select_bitcast_fusion
  282.9 1.3 multiply_convert_fusion
  284.1 0.8 convolution_multiply_fusion
  284.9 4.8 convolution_bitcast_fusion.1
  289.7 0.0 reduce-scatter.9.cloned.1.call-start
  289.8 362.6 %reduce-scatter.7.cloned.1.call-done = f32[64,1]{1,0:T(8,128)} async-done(((f32[4096,1]{1,0:T(8,128)}), f32[64,1]{1,0:T(8,128)}) %reduce-scatter.7.cloned.1.call-update) | async-done | bytes 272
  652.4 0.8 copy.26
  653.2 4.8 convolution_bitcast_fusion
  658.0 0.0 reduce-scatter.9.cloned.1.call-update
  658.0 358.7 %reduce-scatter.9.cloned.1.call-done = f32[64,1]{1,0:T(8,128)} async-done(((f32[4096,1]{1,0:T(8,128)}), f32[64,1]{1,0:T(8,128)}) %reduce-scatter.9.cloned.1.call-update) | async-done | bytes 272
  1016.7 0.8 copy.28
  1017.5 0.5 fusion.14
  (10 shorter events, 0.1 us)
Async XLA Ops:
  7.2 126.6 %all-gather.3.cloned.1.call-start = ((), (), s32[]{:S(2)}) async-start(), calls=%async_computation.2 | async-start | bytes 2263040 | tf_op jit(solution)/shard_map/all_gather | solution.py:52
  13.3 240.3 %all-gather.5.cloned.1.call-start = ((), (), s32[]{:S(2)}) async-start(), calls=%async_computation.3 | async-start | bytes 2263040 | tf_op jit(solution)/shard_map/all_gather | solution.py:55
  19.5 632.9 %reduce-scatter.7.cloned.1.call-start = ((), (), s32[]{:S(2)}) async-start(), calls=%async_computation.4 | async-start | bytes 2129920
  284.1 0.8 copy-start.1
  284.9 368.3 %copy-start = (f32[64,4096]{1,0:T(8,128)}, f32[64,4096]{1,0:T(8,128)S(1)}, u32[]{:S(2)}) copy-start(f32[64,4096]{1,0:T(8,128)S(1)} %convolution_multiply_fusion) | copy-start | bytes 3145732
  289.7 727.0 %reduce-scatter.9.cloned.1.call-start = ((), (), s32[]{:S(2)}) async-start(), calls=%async_computation.5 | async-start | bytes 2129920
Sparse Core Ops, SparseCore 0:
  13.4 120.2 all-gather.2
  137.9 115.6 all-gather.4
  289.8 362.4 reduce-scatter.6
  658.1 358.5 reduce-scatter.8
where the time goes:
time: 1020 us
  waiting for transfers between devices  937 us (92%)
  local copies, waits for them, and re-layouts  46.5 us (5%)
  between operations  15.3 us (2%)
  blocking collectives  10.9 us (1%)
  matrix products  10.3 us (1%)
    unnamed x6, waiting for transfers between devices  721 us
    all_gather x1, waiting for transfers between devices, shards(): lax.all_gather(up_all, 'walker', axis=0, tiled=True)  113 us
    all_gather x1, waiting for transfers between devices, shards(): lax.all_gather(down_all, 'walker', axis=0, tiled=True)  103 us
    reshape x3, local copies, waits for them, and re-layouts, blocks(): return piece.reshape(-1, CLUSTER_MOMENTUM, extent)  37.5 us
  transfers between devices with their start and end apart: 4, of which 4 were waited for; matrix products, arithmetic and copies ran while one was open for 2% of the time, Pallas kernels for 0%

commit v1 on v0

v1 whole, which is shorter than its diff:
```python
import functools
import math

import jax
import jax.numpy as jnp
import numpy as np
from jax import lax
from jax.experimental import pallas as pl
from jax.experimental.pallas import tpu as pltpu
from jax.sharding import Mesh
from jax.sharding import PartitionSpec as P

SIDE = 8
CLUSTER_MOMENTUM = 64
W = 64
NU = 4
ITERS = 2
EXTENT = W + NU - 1
CELLS = CLUSTER_MOMENTUM * W
TAIL = CLUSTER_MOMENTUM * (NU - 1)
GROUP = SIDE * W
UP, DOWN, UP_TAIL, DOWN_TAIL, LOW = 0, CELLS, 2 * CELLS, 2 * CELLS + 256, 2 * CELLS + 512
PACKET = 2 * CELLS + 640
HALF = 128
ROWS = 2 * HALF


def contract(index_ref, own_ref, other_ref, source_ref, g4_ref, out_ref, up, down, left, norm, scale):
    shift_major, shift_minor = index_ref[0] // SIDE, index_ref[0] % SIDE
    offset, site = index_ref[1], index_ref[2]
    halves = (own_ref, other_ref)

    def selector(rows, base, wrapped):
        row = lax.broadcasted_iota(jnp.int32, (rows, GROUP), 0)
        col = lax.broadcasted_iota(jnp.int32, (rows, GROUP), 1)
        minor = (col // W + shift_minor) & (SIDE - 1)
        freq = (col & (W - 1)) + offset
        if wrapped:
            hit = (freq >= W) & (row == base + minor * (NU - 1) + freq - W)
        else:
            hit = (freq < W) & (row == minor * W + freq)
        return hit.astype(jnp.float32).astype(jnp.bfloat16)

    main_select = selector(GROUP, 0, False)

    def build(a, acc):
        moved = (a + shift_major) & (SIDE - 1)
        tail_select = selector(256, moved * SIDE * (NU - 1), True)
        here = pl.ds(pl.multiple_of(a * GROUP, GROUP), GROUP)
        source = source_ref[:, here]
        parts = []
        for half, ref in enumerate(halves):
            rows = pl.ds(half * HALF, HALF)
            for start, tail, held in ((UP, UP_TAIL, up), (DOWN, DOWN_TAIL, down)):
                base = ref[:, pl.ds(pl.multiple_of(start + a * GROUP, GROUP), GROUP)]
                far = ref[:, pl.ds(pl.multiple_of(start + moved * GROUP, GROUP), GROUP)]
                other = jnp.dot(far, main_select, preferred_element_type=jnp.float32)
                other += jnp.dot(
                    ref[:, tail : tail + 256], tail_select, preferred_element_type=jnp.float32
                )
                made = (base.astype(jnp.float32) * other).astype(jnp.bfloat16)
                held[rows, here] = made
                if held is up:
                    weighted = made.astype(jnp.float32) * source
                    parts.append(sum(weighted[:, i : i + 128] for i in range(0, GROUP, 128)))
        return acc + jnp.concatenate(parts, axis=0)

    acc = lax.fori_loop(0, SIDE, build, jnp.zeros((ROWS, 128), jnp.float32))
    first = jnp.sum(acc, axis=1, keepdims=True)

    pair = pl.ds(pl.multiple_of(site // 2 * 128, 128), 128)
    left[...] = up[:, pair].astype(jnp.float32).T
    mine = left[pl.ds(pl.multiple_of(site % 2 * W, W), W), :].astype(jnp.bfloat16)

    def second(a, acc):
        here = pl.ds(pl.multiple_of(a * GROUP, GROUP), GROUP)
        right = down[:, here]
        g4_ref[:, here] = jnp.dot(mine, right, preferred_element_type=jnp.float32) * norm
        moved = jnp.sum(right.astype(jnp.float32) * first, axis=0, keepdims=True)
        current = source_ref[:, here] + (scale * norm) * moved
        weighted = up[:, here].astype(jnp.float32) * current
        return acc + sum(weighted[:, i : i + 128] for i in range(0, GROUP, 128))

    acc = lax.fori_loop(0, SIDE, second, jnp.zeros((ROWS, 128), jnp.float32))
    last = jnp.sum(acc, axis=1, keepdims=True)
    final = source_ref[:, pair] + (scale * norm) * jnp.sum(
        down[:, pair].astype(jnp.float32) * last, axis=0, keepdims=True
    )
    out_ref[...] = jnp.where(site % 2 == 1, final[:, W:], final[:, :W])


def shards(green_up_blocks, green_down_blocks, nu_index, q_index, source):
    samples = ROWS
    norm = 1.0 / math.sqrt(samples)
    scale = 1.0 / (2.0 * math.sqrt(CELLS))

    def split(block):
        sites = block.reshape(CLUSTER_MOMENTUM, EXTENT)
        return sites[:, :W].reshape(CELLS), sites[:, W:].reshape(TAIL)

    up_main, up_tail = split(green_up_blocks)
    down_main, down_tail = split(green_down_blocks)
    start = source.reshape(W)
    high = lax.reduce_precision(start, 8, 7)
    middle = lax.reduce_precision(start - high, 8, 7)
    low = start - high - middle
    packet = jnp.concatenate(
        [
            up_main,
            down_main,
            up_tail,
            high.astype(jnp.bfloat16),
            down_tail,
            middle.astype(jnp.bfloat16),
            low.astype(jnp.bfloat16),
            jnp.zeros((64,), jnp.bfloat16),
        ]
    ).reshape(PACKET // 128, 128)
    along = lax.all_to_all(jnp.broadcast_to(packet, (8,) + packet.shape), "z", 0, 0)
    rows = along.reshape(8, PACKET)
    own = lax.all_to_all(jnp.broadcast_to(rows, (16,) + rows.shape), ("x_hi", "x_lo", "y"), 0, 0)
    own = own.reshape(HALF, PACKET)
    other = lax.ppermute(own, "core", [(0, 1), (1, 0)])
    pieces = own.reshape(2, 2, 32, PACKET)[:, :, :, 2 * CELLS :]
    pieces = lax.dynamic_index_in_dim(pieces, lax.axis_index("x_lo"), 1, False)
    pieces = pieces.reshape(CLUSTER_MOMENTUM, 640).astype(jnp.float32)
    whole = (pieces[:, 192:256] + pieces[:, 448:512]) + pieces[:, 512:576]
    whole = whole.reshape(1, CELLS)
    site = (lax.axis_index("x_hi") * 4 + lax.axis_index("y")) * 8 + lax.axis_index("z")
    index = jnp.stack([q_index[0], nu_index[0], site.astype(jnp.int32)])
    g4, answer = pl.pallas_call(
        functools.partial(contract, norm=norm, scale=scale),
        out_shape=(
            jax.ShapeDtypeStruct((W, CELLS), jnp.float32),
            jax.ShapeDtypeStruct((1, W), jnp.float32),
        ),
        in_specs=[
            pl.BlockSpec(memory_space=pltpu.SMEM),
            pl.BlockSpec(memory_space=pltpu.VMEM),
            pl.BlockSpec(memory_space=pltpu.VMEM),
            pl.BlockSpec(memory_space=pltpu.VMEM),
        ],
        out_specs=(
            pl.BlockSpec(memory_space=pltpu.VMEM),
            pl.BlockSpec(memory_space=pltpu.VMEM),
        ),
        scratch_shapes=[
            pltpu.VMEM((ROWS, CELLS), jnp.bfloat16),
            pltpu.VMEM((ROWS, CELLS), jnp.bfloat16),
            pltpu.VMEM((128, ROWS), jnp.float32),
        ],
        compiler_params=pltpu.CompilerParams(vmem_limit_bytes=48 * 1024 * 1024),
    )(index, own, other, whole)
    return g4.reshape(1, W, CELLS), answer


def solution(mesh):
    fine = Mesh(
        np.asarray(mesh.devices).reshape(2, 4, 8, 2, 2), ("x_hi", "y", "z", "x_lo", "core")
    )
    walker, freq = ("x_hi", "y", "z"), ("x_lo", "core")
    in_specs = (
        P(walker, None, freq, None),
        P(walker, None, freq, None),
        P(freq),
        P(freq),
        P(freq, walker),
    )
    out_specs = (P(freq, walker, None), P(freq, walker))
    return jax.shard_map(shards, mesh=fine, in_specs=in_specs, out_specs=out_specs, check_vma=False)
```

time: 1020 us -> 73.1 us (0.07)
  the two profiles are of different devices: /device:TPU:6 before, /device:TPU:1 now
where the time goes in v1:
time: 73.1 us; the launch traced here: 72.8 us
  blocking collectives  50.2 us (69%)
  Pallas kernels  10.4 us (14%)
  starting transfers between devices  3.92 us (5%)
  waiting for transfers between devices  2.52 us (3%)
  other arithmetic  2.4 us (3%)
  between operations  2 us (3%)
  local copies, waits for them, and re-layouts  1.34 us (2%)
    all_to_all x1, blocking collectives, shards(): lax.all_to_all(jnp.broadcast_to(rows, (16,) + rows.shape), ('x_hi', 'x_lo...  33.5 us
    all_to_all x1, blocking collectives, shards(): lax.all_to_all(jnp.broadcast_to(packet, (8,) + packet.shape), 'z', 0, 0)  16.7 us
    pallas_call x1, Pallas kernels, shards(): pl.pallas_call(functools.partial(contract, norm=norm, scale=scale), out_s...  10.4 us
    ppermute x1, starting transfers between devices, shards(): other = lax.ppermute(own, 'core', [(0, 1), (1, 0)])  3.92 us
    ppermute x1, waiting for transfers between devices, shards(): other = lax.ppermute(own, 'core', [(0, 1), (1, 0)])  2.52 us
    unnamed x2, other arithmetic  1.56 us
  transfers between devices with their start and end apart: 1, of which 1 were waited for; matrix products, arithmetic and copies ran while one was open for 0% of the time, Pallas kernels for 0%

profile of v1, /device:TPU:1, one launch (start us, length us, event | category | flops | bytes accessed | tf_op | source)
XLA Modules:
  0.0 72.8 jit_solution(5866771859636309450)
XLA Ops:
  0.6 0.7 fusion
  1.3 0.8 %reduce = bf16[4288]{0:T(1024)(128)(2,1)S(1)} reduce(bf16[1,1,1,4288]{3,2,1,0:T(2,128)(2,1)} %param.5, bf16[]{:T(256)} %constant.35), dimensions={0,1,2}, to_apply=%param.5.reduce_sub_computation | reduce | bytes 17154 | tf_op args[0]
  2.1 0.2 reshape.44
  2.2 0.1 slice.34
  2.3 0.1 reshape.45
  2.4 0.8 %reduce.1 = bf16[4288]{0:T(1024)(128)(2,1)S(1)} reduce(bf16[1,1,1,4288]{3,2,1,0:T(2,128)(2,1)} %param.6, bf16[]{:T(256)} %constant.35), dimensions={0,1,2}, to_apply=%param.6.reduce_sub_computation | reduce | bytes 17154 | tf_op args[1]
  3.2 0.2 reshape.46
  3.3 0.1 slice.35
  3.4 0.1 reshape.47
  3.5 0.2 reshape.50
  3.6 0.1 reshape.48
  3.8 0.1 concatenate.3
  3.9 16.7 %all_to_all.10 = bf16[8,69,128]{2,1,0:T(8,128)(2,1)S(1)} all-to-all(bf16[8,69,128]{2,1,0:T(8,128)(2,1)S(1)} %broadcast_in_dim.10), channel_id=1, replica_groups=mesh['x_hi'=2,'y'=4,'z'=8,'x_lo'=2,'core'=2] {'z'}, dimensions={0} | all-to-all | bytes 282624 | tf_op jit(solution)/shard_map/all_to_all | solution.py:119
  20.7 0.1 broadcast_in_dim.11
  20.8 33.5 %all_to_all.11 = bf16[16,8,8832]{2,1,0:T(8,128)(2,1)S(1)} all-to-all(bf16[16,8,8832]{2,1,0:T(8,128)(2,1)S(1)} %broadcast_in_dim.11), channel_id=1, replica_groups=mesh['x_hi'=2,'y'=4,'z'=8,'x_lo'=2,'core'=2] {'x_hi','x_lo','y'}, dimensions={0} | all-to-all | bytes 4521984 | tf_op jit(solution)/shard_map/all_to_all | solution.py:121
  54.3 3.9 %collective-permute-start = (bf16[128,8832]{1,0:T(8,128)(2,1)S(1)}, bf16[128,8832]{1,0:T(8,128)(2,1)}, u32[]{:S(2)}, u32[]{:S(2)}) collective-permute-start(bf16[128,8832]{1,0:T(8,128)(2,1)S(1)} %bitcast.23), channel_id=1, source_target_pairs={{0,1},{1,0},{2,3},{3,2},{4,5},{5,4},{6,7},{7,6},{8,9},{9,8},{10,11... | collective-permute-start | bytes 6782984 | tf_op jit(solution)/shard_map/ppermute | solution.py:123
  59.6 0.1 pad_add_fusion.index_ref
  59.7 0.1 slice_add_fusion
  59.8 0.1 reshape.54.source_ref
  59.9 2.5 %collective-permute-done.other_ref = bf16[128,8832]{1,0:T(8,128)(2,1)} collective-permute-done((bf16[128,8832]{1,0:T(8,128)(2,1)S(1)}, bf16[128,8832]{1,0:T(8,128)(2,1)}, u32[]{:S(2)}, u32[]{:S(2)}) %collective-permute-start) | collective-permute-done | bytes 2261024 | tf_op jit(solution)/shard_map/ppermute | solution.py:123
  62.4 10.4 %shard_map.68 = (f32[64,4096]{1,0:T(8,128)}, f32[1,64]{1,0:T(1,128)}) custom-call(s32[3]{0:T(128)S(1)} %pad_add_fusion.index_ref, bf16[128,8832]{1,0:T(8,128)(2,1)S(1)} %bitcast.25, bf16[128,8832]{1,0:T(8,128)(2,1)} %collective-permute-done.other_ref, f32[1,4096]{1,0:T(1,128)S(1)} %reshape.54.source_ref), custom_call_target="tpu_custom_call" | custom-call | tf_op jit(solution)/shard_map/pallas_call | solution.py:131
  (6 shorter events, 0.1 us)
Async XLA Ops:
  54.3 8.1 %collective-permute-start = (bf16[128,8832]{1,0:T(8,128)(2,1)S(1)}, bf16[128,8832]{1,0:T(8,128)(2,1)}, u32[]{:S(2)}, u32[]{:S(2)}) collective-permute-start(bf16[128,8832]{1,0:T(8,128)(2,1)S(1)} %bitcast.23), channel_id=1, source_target_pairs={{0,1},{1,0},{2,3},{3,2},{4,5},{5,4},{6,7},{7,6},{8,9},{9,8},{10,11... | collective-permute-start | bytes 6782984 | tf_op jit(solution)/shard_map/ppermute | solution.py:123

commit v2 on v1

v2 whole, which is shorter than its diff:
```python
import functools
import math

import jax
import jax.numpy as jnp
import numpy as np
from jax import lax
from jax.experimental import pallas as pl
from jax.experimental.pallas import tpu as pltpu
from jax.sharding import Mesh
from jax.sharding import PartitionSpec as P

SIDE = 8
CLUSTER_MOMENTUM = 64
W = 64
NU = 4
ITERS = 2
EXTENT = W + NU - 1
CELLS = CLUSTER_MOMENTUM * W
TAIL = CLUSTER_MOMENTUM * (NU - 1)
GROUP = SIDE * W
UP, DOWN, UP_TAIL, DOWN_TAIL, LOW = 0, CELLS, 2 * CELLS, 2 * CELLS + 256, 2 * CELLS + 512
PACKET = 2 * CELLS + 640
HALF = 128
ROWS = 2 * HALF


def gather_products(index_ref, ref, source_ref, up, down, start_row):
    shift_major, shift_minor = index_ref[0] // SIDE, index_ref[0] % SIDE
    offset = index_ref[1]
    rows = pl.ds(start_row, HALF)

    def selector(count, base, wrapped):
        row = lax.broadcasted_iota(jnp.int32, (count, GROUP), 0)
        col = lax.broadcasted_iota(jnp.int32, (count, GROUP), 1)
        minor = (col // W + shift_minor) & (SIDE - 1)
        freq = (col & (W - 1)) + offset
        if wrapped:
            hit = (freq >= W) & (row == base + minor * (NU - 1) + freq - W)
        else:
            hit = (freq < W) & (row == minor * W + freq)
        return hit.astype(jnp.float32).astype(jnp.bfloat16)

    main_select = selector(GROUP, 0, False)

    def build(a, acc):
        moved = (a + shift_major) & (SIDE - 1)
        tail_select = selector(256, moved * SIDE * (NU - 1), True)
        here = pl.ds(pl.multiple_of(a * GROUP, GROUP), GROUP)
        for start, tail, held in ((UP, UP_TAIL, up), (DOWN, DOWN_TAIL, down)):
            base = ref[:, pl.ds(pl.multiple_of(start + a * GROUP, GROUP), GROUP)]
            far = ref[:, pl.ds(pl.multiple_of(start + moved * GROUP, GROUP), GROUP)]
            other = jnp.dot(far, main_select, preferred_element_type=jnp.float32)
            other += jnp.dot(
                ref[:, tail : tail + 256], tail_select, preferred_element_type=jnp.float32
            )
            made = (base.astype(jnp.float32) * other).astype(jnp.bfloat16)
            held[rows, here] = made
            if held is up:
                weighted = made.astype(jnp.float32) * source_ref[:, here]
                acc = acc + sum(weighted[:, i : i + 128] for i in range(0, GROUP, 128))
        return acc

    return lax.fori_loop(0, SIDE, build, jnp.zeros((HALF, 128), jnp.float32))


def prepare(index_ref, own_ref, source_ref, up_ref, down_ref, sums_ref):
    sums_ref[...] = gather_products(index_ref, own_ref, source_ref, up_ref, down_ref, 0)


def contract(
    index_ref, up_ref, down_ref, sums_ref, other_ref, source_ref, g4_ref, out_ref,
    up_other, down_other, left, norm, scale,
):
    site = index_ref[2]
    sums = gather_products(index_ref, other_ref, source_ref, up_other, down_other, 0)
    first = (
        jnp.sum(sums_ref[...], axis=1, keepdims=True),
        jnp.sum(sums, axis=1, keepdims=True),
    )
    ups, downs = (up_ref, up_other), (down_ref, down_other)

    pair = pl.ds(pl.multiple_of(site // 2 * 128, 128), 128)
    mine = []
    for half, ref in enumerate(ups):
        left[...] = ref[:, pair].astype(jnp.float32).T
        mine.append(left[pl.ds(pl.multiple_of(site % 2 * W, W), W), :].astype(jnp.bfloat16))

    def second(a, acc):
        here = pl.ds(pl.multiple_of(a * GROUP, GROUP), GROUP)
        right = [ref[:, here] for ref in downs]
        g4_ref[:, here] = (
            jnp.dot(mine[0], right[0], preferred_element_type=jnp.float32)
            + jnp.dot(mine[1], right[1], preferred_element_type=jnp.float32)
        ) * norm
        moved = sum(r.astype(jnp.float32) * f for r, f in zip(right, first))
        moved = jnp.sum(moved, axis=0, keepdims=True)
        current = source_ref[:, here] + (scale * norm) * moved
        made = []
        for ref, old in zip(ups, acc):
            weighted = ref[:, here].astype(jnp.float32) * current
            made.append(old + sum(weighted[:, i : i + 128] for i in range(0, GROUP, 128)))
        return tuple(made)

    zero = jnp.zeros((HALF, 128), jnp.float32)
    acc = lax.fori_loop(0, SIDE, second, (zero, zero))
    final = sum(
        ref[:, pair].astype(jnp.float32) * jnp.sum(part, axis=1, keepdims=True)
        for ref, part in zip(downs, acc)
    )
    final = source_ref[:, pair] + (scale * norm) * jnp.sum(final, axis=0, keepdims=True)
    out_ref[...] = jnp.where(site % 2 == 1, final[:, W:], final[:, :W])


def shards(green_up_blocks, green_down_blocks, nu_index, q_index, source):
    samples = ROWS
    norm = 1.0 / math.sqrt(samples)
    scale = 1.0 / (2.0 * math.sqrt(CELLS))

    both = jnp.concatenate(
        [green_up_blocks.reshape(1, -1), green_down_blocks.reshape(1, -1)], axis=0
    )
    sites = both.reshape(2 * CLUSTER_MOMENTUM, EXTENT)
    main = sites[:, :W].reshape(2 * CELLS)
    tails = sites[:, W:].reshape(2, TAIL)
    up_tail, down_tail = tails[0], tails[1]
    start = source.reshape(W)
    high = lax.reduce_precision(start, 8, 7)
    middle = lax.reduce_precision(start - high, 8, 7)
    low = start - high - middle
    packet = jnp.concatenate(
        [
            main,
            up_tail,
            high.astype(jnp.bfloat16),
            down_tail,
            middle.astype(jnp.bfloat16),
            low.astype(jnp.bfloat16),
            jnp.zeros((64,), jnp.bfloat16),
        ]
    ).reshape(PACKET // 128, 128)
    along = lax.all_to_all(jnp.broadcast_to(packet, (8,) + packet.shape), "z", 0, 0)
    rows = along.reshape(8, PACKET)
    own = lax.all_to_all(jnp.broadcast_to(rows, (16,) + rows.shape), ("x_hi", "x_lo", "y"), 0, 0)
    own = own.reshape(HALF, PACKET)
    other = lax.ppermute(own, "core", [(0, 1), (1, 0)])
    pieces = own.reshape(2, 2, 32, PACKET)[:, :, :, 2 * CELLS :]
    pieces = lax.dynamic_index_in_dim(pieces, lax.axis_index("x_lo"), 1, False)
    pieces = pieces.reshape(CLUSTER_MOMENTUM, 640).astype(jnp.float32)
    whole = (pieces[:, 192:256] + pieces[:, 448:512]) + pieces[:, 512:576]
    whole = whole.reshape(1, CELLS)
    site = (lax.axis_index("x_hi") * 4 + lax.axis_index("y")) * 8 + lax.axis_index("z")
    index = jnp.stack([q_index[0], nu_index[0], site.astype(jnp.int32)])
    vmem = pl.BlockSpec(memory_space=pltpu.VMEM)
    smem = pl.BlockSpec(memory_space=pltpu.SMEM)
    limit = pltpu.CompilerParams(vmem_limit_bytes=48 * 1024 * 1024)
    up, down, sums = pl.pallas_call(
        prepare,
        out_shape=(
            jax.ShapeDtypeStruct((HALF, CELLS), jnp.bfloat16),
            jax.ShapeDtypeStruct((HALF, CELLS), jnp.bfloat16),
            jax.ShapeDtypeStruct((HALF, 128), jnp.float32),
        ),
        in_specs=[smem, vmem, vmem],
        out_specs=(vmem, vmem, vmem),
        compiler_params=limit,
    )(index, own, whole)
    g4, answer = pl.pallas_call(
        functools.partial(contract, norm=norm, scale=scale),
        out_shape=(
            jax.ShapeDtypeStruct((W, CELLS), jnp.float32),
            jax.ShapeDtypeStruct((1, W), jnp.float32),
        ),
        in_specs=[smem, vmem, vmem, vmem, vmem, vmem],
        out_specs=(vmem, vmem),
        scratch_shapes=[
            pltpu.VMEM((HALF, CELLS), jnp.bfloat16),
            pltpu.VMEM((HALF, CELLS), jnp.bfloat16),
            pltpu.VMEM((128, HALF), jnp.float32),
        ],
        compiler_params=limit,
    )(index, up, down, sums, other, whole)
    return g4.reshape(1, W, CELLS), answer


def solution(mesh):
    fine = Mesh(
        np.asarray(mesh.devices).reshape(2, 4, 8, 2, 2), ("x_hi", "y", "z", "x_lo", "core")
    )
    walker, freq = ("x_hi", "y", "z"), ("x_lo", "core")
    in_specs = (
        P(walker, None, freq, None),
        P(walker, None, freq, None),
        P(freq),
        P(freq),
        P(freq, walker),
    )
    out_specs = (P(freq, walker, None), P(freq, walker))
    return jax.shard_map(shards, mesh=fine, in_specs=in_specs, out_specs=out_specs, check_vma=False)
```

time: 73.1 us -> 71.6 us (0.979)
  waiting for transfers between devices: 2.52 us -> 0.01 us
  Pallas kernels: 10.4 us -> 12.5 us
  other arithmetic: 2.4 us -> 1.62 us
    pallas_call x0 -> x1, Pallas kernels: none -> 4.15 us  [shards(): pl.pallas_call(prepare, out_shape=(jax.ShapeDtypeStruct((HALF, CELLS), jn...]
    ppermute x1, waiting for transfers between devices: 2.52 us -> 0.01 us  [shards(): other = lax.ppermute(own, 'core', [(0, 1), (1, 0)])]
    pallas_call x1, Pallas kernels: 10.4 us -> 8.31 us  [shards(): pl.pallas_call(functools.partial(contract, norm=norm, scale=scale), out_s...]
    unnamed x2 -> x0, other arithmetic: 1.56 us -> none
    concatenate x0 -> x1, other arithmetic: none -> 0.78 us  [shards(): jnp.concatenate([green_up_blocks.reshape(1, -1), green_down_blocks.reshap...]
  transfers between devices with their start and end apart: 1 -> 1, of which waited for: 1 -> 0; matrix products, arithmetic and copies ran while one was open for 0% -> 0% of each run, Pallas kernels for 0% -> 6%
where the time goes in v2:
time: 71.6 us; the launch traced here: 71.3 us
  blocking collectives  50.2 us (70%)
  Pallas kernels  12.5 us (17%)
  starting transfers between devices  3.92 us (5%)
  between operations  2.02 us (3%)
  other arithmetic  1.62 us (2%)
  local copies, waits for them, and re-layouts  1.02 us (1%)
    all_to_all x1, blocking collectives, shards(): lax.all_to_all(jnp.broadcast_to(rows, (16,) + rows.shape), ('x_hi', 'x_lo...  33.5 us
    all_to_all x1, blocking collectives, shards(): lax.all_to_all(jnp.broadcast_to(packet, (8,) + packet.shape), 'z', 0, 0)  16.7 us
    pallas_call x1, Pallas kernels, shards(): pl.pallas_call(functools.partial(contract, norm=norm, scale=scale), out_s...  8.31 us
    pallas_call x1, Pallas kernels, shards(): pl.pallas_call(prepare, out_shape=(jax.ShapeDtypeStruct((HALF, CELLS), jn...  4.15 us
    ppermute x1, starting transfers between devices, shards(): other = lax.ppermute(own, 'core', [(0, 1), (1, 0)])  3.92 us
  transfers between devices with their start and end apart: 1, of which 0 were waited for; matrix products, arithmetic and copies ran while one was open for 0% of the time, Pallas kernels for 6%

profile of v2, /device:TPU:1, one launch (start us, length us, event | category | flops | bytes accessed | tf_op | source)
XLA Modules:
  0.0 71.3 jit_solution(11667089373257006750)
XLA Ops:
  0.6 0.7 fusion
  1.3 0.8 %pad_maximum_fusion = bf16[2,4288]{1,0:T(2,128)(2,1)S(1)} fusion(bf16[1,4288]{1,0:T(2,128)(2,1)} %bitcast.31, bf16[1,4288]{1,0:T(2,128)(2,1)} %bitcast.32), kind=kLoop, calls=%fused_computation.4 | loop fusion | flops 34304 | bytes 34304 | tf_op jit(solution)/shard_map/concatenate | solution.py:120
  2.1 0.2 reshape.45
  2.2 0.1 fusion.1
  2.3 0.1 reshape.46
  2.4 0.1 squeeze.9
  2.6 0.1 squeeze.8
  2.7 0.1 concatenate.7
  2.8 16.7 %all_to_all.10 = bf16[8,69,128]{2,1,0:T(8,128)(2,1)S(1)} all-to-all(bf16[8,69,128]{2,1,0:T(8,128)(2,1)S(1)} %broadcast_in_dim.10), channel_id=1, replica_groups=mesh['x_hi'=2,'y'=4,'z'=8,'x_lo'=2,'core'=2] {'z'}, dimensions={0} | all-to-all | bytes 282624 | tf_op jit(solution)/shard_map/all_to_all | solution.py:142
  19.6 0.1 broadcast_in_dim.11
  19.7 33.5 %all_to_all.11 = bf16[16,8,8832]{2,1,0:T(8,128)(2,1)S(1)} all-to-all(bf16[16,8,8832]{2,1,0:T(8,128)(2,1)S(1)} %broadcast_in_dim.11), channel_id=1, replica_groups=mesh['x_hi'=2,'y'=4,'z'=8,'x_lo'=2,'core'=2] {'x_hi','x_lo','y'}, dimensions={0} | all-to-all | bytes 4521984 | tf_op jit(solution)/shard_map/all_to_all | solution.py:144
  53.3 3.9 %collective-permute-start = (bf16[128,8832]{1,0:T(8,128)(2,1)S(1)}, bf16[128,8832]{1,0:T(8,128)(2,1)}, u32[]{:S(2)}, u32[]{:S(2)}) collective-permute-start(bf16[128,8832]{1,0:T(8,128)(2,1)S(1)} %bitcast.24), channel_id=1, source_target_pairs={{0,1},{1,0},{2,3},{3,2},{4,5},{5,4},{6,7},{7,6},{8,9},{9,8},{10,11... | collective-permute-start | bytes 6782984 | tf_op jit(solution)/shard_map/ppermute | solution.py:146
  58.5 0.1 pad_add_fusion.index_ref
  58.6 0.1 slice_add_fusion
  58.7 0.1 reshape.51.source_ref
  58.8 4.2 %shard_map.68 = (bf16[128,4096]{1,0:T(8,128)(2,1)S(1)}, bf16[128,4096]{1,0:T(8,128)(2,1)S(1)}, f32[128,128]{1,0:T(8,128)S(1)}) custom-call(s32[3]{0:T(128)S(1)} %pad_add_fusion.index_ref, bf16[128,8832]{1,0:T(8,128)(2,1)S(1)} %bitcast.26, f32[1,4096]{1,0:T(1,128)S(1)} %reshape.51.source_ref), custom_call_target="tpu_custom_call" | custom-call | tf_op jit(solution)/shard_map/pallas_call | solution.py:157
  63.0 0.0 collective-permute-done.other_ref
  63.0 8.3 %shard_map.69 = (f32[64,4096]{1,0:T(8,128)}, f32[1,64]{1,0:T(1,128)}) custom-call(s32[3]{0:T(128)S(1)} %pad_add_fusion.index_ref, bf16[128,4096]{1,0:T(8,128)(2,1)S(1)} %get-tuple-element.7.up_ref, bf16[128,4096]{1,0:T(8,128)(2,1)S(1)} %get-tuple-element.8.down_ref, f32[128,128]{1,0:T(8,128)S(1)} %get-tuple-element.9.sums_ref, ...), custom_call_target="tpu_custom_call" | custom-call | tf_op jit(solution)/shard_map/pallas_call | solution.py:168
  (6 shorter events, 0.1 us)
Async XLA Ops:
  53.3 9.7 %collective-permute-start = (bf16[128,8832]{1,0:T(8,128)(2,1)S(1)}, bf16[128,8832]{1,0:T(8,128)(2,1)}, u32[]{:S(2)}, u32[]{:S(2)}) collective-permute-start(bf16[128,8832]{1,0:T(8,128)(2,1)S(1)} %bitcast.24), channel_id=1, source_target_pairs={{0,1},{1,0},{2,3},{3,2},{4,5},{5,4},{6,7},{7,6},{8,9},{9,8},{10,11... | collective-permute-start | bytes 6782984 | tf_op jit(solution)/shard_map/ppermute | solution.py:146

commit v3 on v2

--- a/solution.py
+++ b/solution.py
@@ -30,35 +30,40 @@
     offset = index_ref[1]
     rows = pl.ds(start_row, HALF)
 
-    def selector(count, base, wrapped):
-        row = lax.broadcasted_iota(jnp.int32, (count, GROUP), 0)
-        col = lax.broadcasted_iota(jnp.int32, (count, GROUP), 1)
-        minor = (col // W + shift_minor) & (SIDE - 1)
-        freq = (col & (W - 1)) + offset
-        if wrapped:
-            hit = (freq >= W) & (row == base + minor * (NU - 1) + freq - W)
-        else:
-            hit = (freq < W) & (row == minor * W + freq)
-        return hit.astype(jnp.float32).astype(jnp.bfloat16)
-
-    main_select = selector(GROUP, 0, False)
+    lanes = shift_minor * W + offset
+    tiles, inner = lanes // 128, lanes % 128
+    lane = lax.broadcasted_iota(jnp.int32, (HALF, 128), 1)
+    near = lane + inner < 128
+    kept = (lane & (W - 1)) + offset < W
+
+    col = lax.broadcasted_iota(jnp.int32, (1, GROUP), 1)
+    freq = (col & (W - 1)) + offset
+    minor = (col // W + shift_minor) & (SIDE - 1)
+    wanted = jnp.where(freq >= W, minor * (NU - 1) + freq - W, -256)
+    row = lax.broadcasted_iota(jnp.int32, (256, GROUP), 0)
 
     def build(a, acc):
         moved = (a + shift_major) & (SIDE - 1)
-        tail_select = selector(256, moved * SIDE * (NU - 1), True)
-        here = pl.ds(pl.multiple_of(a * GROUP, GROUP), GROUP)
+        tail_select = jnp.where(row == wanted + moved * SIDE * (NU - 1), 1.0, 0.0)
+        tail_select = tail_select.astype(jnp.bfloat16)
         for start, tail, held in ((UP, UP_TAIL, up), (DOWN, DOWN_TAIL, down)):
-            base = ref[:, pl.ds(pl.multiple_of(start + a * GROUP, GROUP), GROUP)]
-            far = ref[:, pl.ds(pl.multiple_of(start + moved * GROUP, GROUP), GROUP)]
-            other = jnp.dot(far, main_select, preferred_element_type=jnp.float32)
-            other += jnp.dot(
+            wrapped = jnp.dot(
                 ref[:, tail : tail + 256], tail_select, preferred_element_type=jnp.float32
             )
-            made = (base.astype(jnp.float32) * other).astype(jnp.bfloat16)
-            held[rows, here] = made
-            if held is up:
-                weighted = made.astype(jnp.float32) * source_ref[:, here]
-                acc = acc + sum(weighted[:, i : i + 128] for i in range(0, GROUP, 128))
+            turned = []
+            for t in range(GROUP // 128):
+                begin = start + moved * GROUP + ((t + tiles) & (GROUP // 128 - 1)) * 128
+                far = ref[:, pl.ds(pl.multiple_of(begin, 128), 128)].astype(jnp.float32)
+                turned.append(pltpu.roll(far, (128 - inner) & 127, 1))
+            for t in range(GROUP // 128):
+                here = pl.ds(pl.multiple_of(a * GROUP + t * 128, 128), 128)
+                base = ref[:, pl.ds(pl.multiple_of(start + a * GROUP + t * 128, 128), 128)]
+                other = jnp.where(near, turned[t], turned[(t + 1) % len(turned)])
+                other = jnp.where(kept, other, wrapped[:, t * 128 : t * 128 + 128])
+                made = (base.astype(jnp.float32) * other).astype(jnp.bfloat16)
+                held[rows, here] = made
+                if held is up:
+                    acc = acc + made.astype(jnp.float32) * source_ref[:, here]
         return acc
 
     return lax.fori_loop(0, SIDE, build, jnp.zeros((HALF, 128), jnp.float32))

time: 71.6 us -> 70.4 us (0.983)
  Pallas kernels: 12.5 us -> 11.3 us
  transfers between devices with their start and end apart: 1 -> 1, of which waited for: 0 -> 0; matrix products, arithmetic and copies ran while one was open for 0% -> 0% of each run, Pallas kernels for 6% -> 5%
where the time goes in v3:
time: 70.4 us; the launch traced here: 70.1 us
  blocking collectives  50.2 us (71%)
  Pallas kernels  11.3 us (16%)
  starting transfers between devices  3.92 us (6%)
  between operations  2.02 us (3%)
  other arithmetic  1.62 us (2%)
  local copies, waits for them, and re-layouts  1.02 us (1%)
    all_to_all x1, blocking collectives, shards(): lax.all_to_all(jnp.broadcast_to(rows, (16,) + rows.shape), ('x_hi', 'x_lo...  33.5 us
    all_to_all x1, blocking collectives, shards(): lax.all_to_all(jnp.broadcast_to(packet, (8,) + packet.shape), 'z', 0, 0)  16.7 us
    pallas_call x1, Pallas kernels, shards(): pl.pallas_call(functools.partial(contract, norm=norm, scale=scale), out_s...  7.71 us
    ppermute x1, starting transfers between devices, shards(): other = lax.ppermute(own, 'core', [(0, 1), (1, 0)])  3.92 us
    pallas_call x1, Pallas kernels, shards(): pl.pallas_call(prepare, out_shape=(jax.ShapeDtypeStruct((HALF, CELLS), jn...  3.59 us
  transfers between devices with their start and end apart: 1, of which 0 were waited for; matrix products, arithmetic and copies ran while one was open for 0% of the time, Pallas kernels for 5%

profile of v3, /device:TPU:1, one launch (start us, length us, event | category | flops | bytes accessed | tf_op | source)
XLA Modules:
  0.0 70.1 jit_solution(3674970836921842304)
XLA Ops:
  0.6 0.7 fusion
  1.3 0.8 %pad_maximum_fusion = bf16[2,4288]{1,0:T(2,128)(2,1)S(1)} fusion(bf16[1,4288]{1,0:T(2,128)(2,1)} %bitcast.31, bf16[1,4288]{1,0:T(2,128)(2,1)} %bitcast.32), kind=kLoop, calls=%fused_computation.4 | loop fusion | flops 34304 | bytes 34304 | tf_op jit(solution)/shard_map/concatenate | solution.py:125
  2.1 0.2 reshape.45
  2.2 0.1 fusion.1
  2.3 0.1 reshape.46
  2.4 0.1 squeeze.9
  2.6 0.1 squeeze.8
  2.7 0.1 concatenate.7
  2.8 16.7 %all_to_all.10 = bf16[8,69,128]{2,1,0:T(8,128)(2,1)S(1)} all-to-all(bf16[8,69,128]{2,1,0:T(8,128)(2,1)S(1)} %broadcast_in_dim.10), channel_id=1, replica_groups=mesh['x_hi'=2,'y'=4,'z'=8,'x_lo'=2,'core'=2] {'z'}, dimensions={0} | all-to-all | bytes 282624 | tf_op jit(solution)/shard_map/all_to_all | solution.py:147
  19.6 0.1 broadcast_in_dim.11
  19.7 33.5 %all_to_all.11 = bf16[16,8,8832]{2,1,0:T(8,128)(2,1)S(1)} all-to-all(bf16[16,8,8832]{2,1,0:T(8,128)(2,1)S(1)} %broadcast_in_dim.11), channel_id=1, replica_groups=mesh['x_hi'=2,'y'=4,'z'=8,'x_lo'=2,'core'=2] {'x_hi','x_lo','y'}, dimensions={0} | all-to-all | bytes 4521984 | tf_op jit(solution)/shard_map/all_to_all | solution.py:149
  53.3 3.9 %collective-permute-start = (bf16[128,8832]{1,0:T(8,128)(2,1)S(1)}, bf16[128,8832]{1,0:T(8,128)(2,1)}, u32[]{:S(2)}, u32[]{:S(2)}) collective-permute-start(bf16[128,8832]{1,0:T(8,128)(2,1)S(1)} %bitcast.24), channel_id=1, source_target_pairs={{0,1},{1,0},{2,3},{3,2},{4,5},{5,4},{6,7},{7,6},{8,9},{9,8},{10,11... | collective-permute-start | bytes 6782984 | tf_op jit(solution)/shard_map/ppermute | solution.py:151
  58.5 0.1 pad_add_fusion.index_ref
  58.6 0.1 slice_add_fusion
  58.7 0.1 reshape.51.source_ref
  58.8 3.6 %shard_map.68 = (bf16[128,4096]{1,0:T(8,128)(2,1)S(1)}, bf16[128,4096]{1,0:T(8,128)(2,1)S(1)}, f32[128,128]{1,0:T(8,128)S(1)}) custom-call(s32[3]{0:T(128)S(1)} %pad_add_fusion.index_ref, bf16[128,8832]{1,0:T(8,128)(2,1)S(1)} %bitcast.26, f32[1,4096]{1,0:T(1,128)S(1)} %reshape.51.source_ref), custom_call_target="tpu_custom_call" | custom-call | tf_op jit(solution)/shard_map/pallas_call | solution.py:162
  62.4 0.0 collective-permute-done.other_ref
  62.4 7.7 %shard_map.69 = (f32[64,4096]{1,0:T(8,128)}, f32[1,64]{1,0:T(1,128)}) custom-call(s32[3]{0:T(128)S(1)} %pad_add_fusion.index_ref, bf16[128,4096]{1,0:T(8,128)(2,1)S(1)} %get-tuple-element.7.up_ref, bf16[128,4096]{1,0:T(8,128)(2,1)S(1)} %get-tuple-element.8.down_ref, f32[128,128]{1,0:T(8,128)S(1)} %get-tuple-element.9.sums_ref, ...), custom_call_target="tpu_custom_call" | custom-call | tf_op jit(solution)/shard_map/pallas_call | solution.py:173
  (6 shorter events, 0.1 us)
Async XLA Ops:
  53.3 9.2 %collective-permute-start = (bf16[128,8832]{1,0:T(8,128)(2,1)S(1)}, bf16[128,8832]{1,0:T(8,128)(2,1)}, u32[]{:S(2)}, u32[]{:S(2)}) collective-permute-start(bf16[128,8832]{1,0:T(8,128)(2,1)S(1)} %bitcast.24), channel_id=1, source_target_pairs={{0,1},{1,0},{2,3},{3,2},{4,5},{5,4},{6,7},{7,6},{8,9},{9,8},{10,11... | collective-permute-start | bytes 6782984 | tf_op jit(solution)/shard_map/ppermute | solution.py:151

commit v4 on v3

--- a/solution.py
+++ b/solution.py
@@ -73,48 +73,62 @@
     sums_ref[...] = gather_products(index_ref, own_ref, source_ref, up_ref, down_ref, 0)
 
 
+def three_rows(row):
+    high = row.astype(jnp.bfloat16).astype(jnp.float32)
+    middle = (row - high).astype(jnp.bfloat16).astype(jnp.float32)
+    low = row - high - middle
+    at = lax.broadcasted_iota(jnp.int32, (16, row.shape[1]), 0)
+    return jnp.where(
+        at == 0, high, jnp.where(at == 1, middle, jnp.where(at == 2, low, 0.0))
+    )
+
+
 def contract(
     index_ref, up_ref, down_ref, sums_ref, other_ref, source_ref, g4_ref, out_ref,
-    up_other, down_other, left, norm, scale,
+    up_other, down_other, left, stage, sems, norm, scale,
 ):
     site = index_ref[2]
     sums = gather_products(index_ref, other_ref, source_ref, up_other, down_other, 0)
-    first = (
-        jnp.sum(sums_ref[...], axis=1, keepdims=True),
-        jnp.sum(sums, axis=1, keepdims=True),
+    first = jnp.concatenate(
+        [jnp.sum(part.T, axis=0, keepdims=True) for part in (sums_ref[...], sums)], axis=1
     )
     ups, downs = (up_ref, up_other), (down_ref, down_other)
 
     pair = pl.ds(pl.multiple_of(site // 2 * 128, 128), 128)
     mine = []
-    for half, ref in enumerate(ups):
+    for ref in ups:
         left[...] = ref[:, pair].astype(jnp.float32).T
-        mine.append(left[pl.ds(pl.multiple_of(site % 2 * W, W), W), :].astype(jnp.bfloat16))
-
-    def second(a, acc):
-        here = pl.ds(pl.multiple_of(a * GROUP, GROUP), GROUP)
-        right = [ref[:, here] for ref in downs]
-        g4_ref[:, here] = (
-            jnp.dot(mine[0], right[0], preferred_element_type=jnp.float32)
-            + jnp.dot(mine[1], right[1], preferred_element_type=jnp.float32)
-        ) * norm
-        moved = sum(r.astype(jnp.float32) * f for r, f in zip(right, first))
-        moved = jnp.sum(moved, axis=0, keepdims=True)
+        mine.append(left[pl.ds(pl.multiple_of(site % 2 * W, W), W), :])
+    lhs = jnp.concatenate([jnp.concatenate(mine, axis=1), three_rows(first)], axis=0)
+    lhs = lhs.astype(jnp.bfloat16)
+
+    copies = []
+    last = [jnp.zeros((16, HALF), jnp.float32), jnp.zeros((16, HALF), jnp.float32)]
+    for a in range(SIDE):
+        here = pl.ds(a * GROUP, GROUP)
+        right = jnp.concatenate([ref[:, here] for ref in downs], axis=0)
+        both = jnp.dot(lhs, right, preferred_element_type=jnp.float32)
+        stage[:, here] = both[:W] * norm
+        copies.append(
+            pltpu.make_async_copy(stage.at[:, here], g4_ref.at[:, here], sems.at[a])
+        )
+        copies[-1].start()
+        moved = jnp.sum(both[W:], axis=0, keepdims=True)
         current = source_ref[:, here] + (scale * norm) * moved
-        made = []
-        for ref, old in zip(ups, acc):
-            weighted = ref[:, here].astype(jnp.float32) * current
-            made.append(old + sum(weighted[:, i : i + 128] for i in range(0, GROUP, 128)))
-        return tuple(made)
-
-    zero = jnp.zeros((HALF, 128), jnp.float32)
-    acc = lax.fori_loop(0, SIDE, second, (zero, zero))
-    final = sum(
-        ref[:, pair].astype(jnp.float32) * jnp.sum(part, axis=1, keepdims=True)
-        for ref, part in zip(downs, acc)
-    )
+        rows = three_rows(current).astype(jnp.bfloat16)
+        for half, ref in enumerate(ups):
+            last[half] += lax.dot_general(
+                rows, ref[:, here], (((1,), (1,)), ((), ())),
+                preferred_element_type=jnp.float32,
+            )
+    final = jnp.zeros((16, 128), jnp.float32)
+    for part, ref in zip(last, downs):
+        rows = three_rows(jnp.sum(part, axis=0, keepdims=True)).astype(jnp.bfloat16)
+        final += jnp.dot(rows, ref[:, pair], preferred_element_type=jnp.float32)
     final = source_ref[:, pair] + (scale * norm) * jnp.sum(final, axis=0, keepdims=True)
     out_ref[...] = jnp.where(site % 2 == 1, final[:, W:], final[:, :W])
+    for copy in copies:
+        copy.wait()
 
 
 def shards(green_up_blocks, green_down_blocks, nu_index, q_index, source):
@@ -177,11 +191,13 @@
             jax.ShapeDtypeStruct((1, W), jnp.float32),
         ),
         in_specs=[smem, vmem, vmem, vmem, vmem, vmem],
-        out_specs=(vmem, vmem),
+        out_specs=(pl.BlockSpec(memory_space=pl.ANY), vmem),
         scratch_shapes=[
             pltpu.VMEM((HALF, CELLS), jnp.bfloat16),
             pltpu.VMEM((HALF, CELLS), jnp.bfloat16),
             pltpu.VMEM((128, HALF), jnp.float32),
+            pltpu.VMEM((W, CELLS), jnp.float32),
+            pltpu.SemaphoreType.DMA((SIDE,)),
         ],
         compiler_params=limit,
     )(index, up, down, sums, other, whole)

time: 70.4 us -> 70.5 us (level)
  no operation moved by 1% of the time
where the time goes in v4:
time: 70.5 us; the launch traced here: 70.2 us
  blocking collectives  50.2 us (71%)
  Pallas kernels  11.4 us (16%)
  starting transfers between devices  3.92 us (6%)
  between operations  2.02 us (3%)
  other arithmetic  1.62 us (2%)
  local copies, waits for them, and re-layouts  1.02 us (1%)
    all_to_all x1, blocking collectives, shards(): lax.all_to_all(jnp.broadcast_to(rows, (16,) + rows.shape), ('x_hi', 'x_lo...  33.5 us
    all_to_all x1, blocking collectives, shards(): lax.all_to_all(jnp.broadcast_to(packet, (8,) + packet.shape), 'z', 0, 0)  16.7 us
    pallas_call x1, Pallas kernels, shards(): pl.pallas_call(functools.partial(contract, norm=norm, scale=scale), out_s...  7.79 us
    ppermute x1, starting transfers between devices, shards(): other = lax.ppermute(own, 'core', [(0, 1), (1, 0)])  3.92 us
    pallas_call x1, Pallas kernels, shards(): pl.pallas_call(prepare, out_shape=(jax.ShapeDtypeStruct((HALF, CELLS), jn...  3.59 us
  transfers between devices with their start and end apart: 1, of which 0 were waited for; matrix products, arithmetic and copies ran while one was open for 0% of the time, Pallas kernels for 5%

profile of v4, /device:TPU:1, one launch (start us, length us, event | category | flops | bytes accessed | tf_op | source)
XLA Modules:
  0.0 70.2 jit_solution(4499566827361782652)
XLA Ops:
  0.6 0.7 fusion
  1.3 0.8 %pad_maximum_fusion = bf16[2,4288]{1,0:T(2,128)(2,1)S(1)} fusion(bf16[1,4288]{1,0:T(2,128)(2,1)} %bitcast.31, bf16[1,4288]{1,0:T(2,128)(2,1)} %bitcast.32), kind=kLoop, calls=%fused_computation.4 | loop fusion | flops 34304 | bytes 34304 | tf_op jit(solution)/shard_map/concatenate | solution.py:139
  2.1 0.2 reshape.45
  2.2 0.1 fusion.1
  2.3 0.1 reshape.46
  2.4 0.1 squeeze.9
  2.6 0.1 squeeze.8
  2.7 0.1 concatenate.7
  2.8 16.7 %all_to_all.10 = bf16[8,69,128]{2,1,0:T(8,128)(2,1)S(1)} all-to-all(bf16[8,69,128]{2,1,0:T(8,128)(2,1)S(1)} %broadcast_in_dim.10), channel_id=1, replica_groups=mesh['x_hi'=2,'y'=4,'z'=8,'x_lo'=2,'core'=2] {'z'}, dimensions={0} | all-to-all | bytes 282624 | tf_op jit(solution)/shard_map/all_to_all | solution.py:161
  19.6 0.1 broadcast_in_dim.11
  19.7 33.5 %all_to_all.11 = bf16[16,8,8832]{2,1,0:T(8,128)(2,1)S(1)} all-to-all(bf16[16,8,8832]{2,1,0:T(8,128)(2,1)S(1)} %broadcast_in_dim.11), channel_id=1, replica_groups=mesh['x_hi'=2,'y'=4,'z'=8,'x_lo'=2,'core'=2] {'x_hi','x_lo','y'}, dimensions={0} | all-to-all | bytes 4521984 | tf_op jit(solution)/shard_map/all_to_all | solution.py:163
  53.3 3.9 %collective-permute-start = (bf16[128,8832]{1,0:T(8,128)(2,1)S(1)}, bf16[128,8832]{1,0:T(8,128)(2,1)}, u32[]{:S(2)}, u32[]{:S(2)}) collective-permute-start(bf16[128,8832]{1,0:T(8,128)(2,1)S(1)} %bitcast.24), channel_id=1, source_target_pairs={{0,1},{1,0},{2,3},{3,2},{4,5},{5,4},{6,7},{7,6},{8,9},{9,8},{10,11... | collective-permute-start | bytes 6782984 | tf_op jit(solution)/shard_map/ppermute | solution.py:165
  58.5 0.1 pad_add_fusion.index_ref
  58.6 0.1 slice_add_fusion
  58.7 0.1 reshape.51.source_ref
  58.8 3.6 %shard_map.68 = (bf16[128,4096]{1,0:T(8,128)(2,1)S(1)}, bf16[128,4096]{1,0:T(8,128)(2,1)S(1)}, f32[128,128]{1,0:T(8,128)S(1)}) custom-call(s32[3]{0:T(128)S(1)} %pad_add_fusion.index_ref, bf16[128,8832]{1,0:T(8,128)(2,1)S(1)} %bitcast.26, f32[1,4096]{1,0:T(1,128)S(1)} %reshape.51.source_ref), custom_call_target="tpu_custom_call" | custom-call | tf_op jit(solution)/shard_map/pallas_call | solution.py:176
  62.4 0.0 collective-permute-done.other_ref
  62.4 7.8 %shard_map.69 = (f32[64,4096]{1,0:T(8,128)}, f32[1,64]{1,0:T(1,128)}) custom-call(s32[3]{0:T(128)S(1)} %pad_add_fusion.index_ref, bf16[128,4096]{1,0:T(8,128)(2,1)S(1)} %get-tuple-element.7.up_ref, bf16[128,4096]{1,0:T(8,128)(2,1)S(1)} %get-tuple-element.8.down_ref, f32[128,128]{1,0:T(8,128)S(1)} %get-tuple-element.9.sums_ref, ...), custom_call_target="tpu_custom_call" | custom-call | tf_op jit(solution)/shard_map/pallas_call | solution.py:187
  (6 shorter events, 0.1 us)
Async XLA Ops:
  53.3 9.2 %collective-permute-start = (bf16[128,8832]{1,0:T(8,128)(2,1)S(1)}, bf16[128,8832]{1,0:T(8,128)(2,1)}, u32[]{:S(2)}, u32[]{:S(2)}) collective-permute-start(bf16[128,8832]{1,0:T(8,128)(2,1)S(1)} %bitcast.24), channel_id=1, source_target_pairs={{0,1},{1,0},{2,3},{3,2},{4,5},{5,4},{6,7},{7,6},{8,9},{9,8},{10,11... | collective-permute-start | bytes 6782984 | tf_op jit(solution)/shard_map/ppermute | solution.py:165

commit v5 on v4

--- a/solution.py
+++ b/solution.py
@@ -25,10 +25,10 @@
 ROWS = 2 * HALF
 
 
-def gather_products(index_ref, ref, source_ref, up, down, start_row):
+def gather_products(index_ref, ref, source_ref, up, down, stages):
     shift_major, shift_minor = index_ref[0] // SIDE, index_ref[0] % SIDE
     offset = index_ref[1]
-    rows = pl.ds(start_row, HALF)
+    spins = ((UP, UP_TAIL, up), (DOWN, DOWN_TAIL, down))
 
     lanes = shift_minor * W + offset
     tiles, inner = lanes // 128, lanes % 128
@@ -42,11 +42,11 @@
     wanted = jnp.where(freq >= W, minor * (NU - 1) + freq - W, -256)
     row = lax.broadcasted_iota(jnp.int32, (256, GROUP), 0)
 
-    def build(a, acc):
+    def build(chosen, a, acc):
         moved = (a + shift_major) & (SIDE - 1)
         tail_select = jnp.where(row == wanted + moved * SIDE * (NU - 1), 1.0, 0.0)
         tail_select = tail_select.astype(jnp.bfloat16)
-        for start, tail, held in ((UP, UP_TAIL, up), (DOWN, DOWN_TAIL, down)):
+        for start, tail, held in chosen:
             wrapped = jnp.dot(
                 ref[:, tail : tail + 256], tail_select, preferred_element_type=jnp.float32
             )
@@ -61,16 +61,22 @@
                 other = jnp.where(near, turned[t], turned[(t + 1) % len(turned)])
                 other = jnp.where(kept, other, wrapped[:, t * 128 : t * 128 + 128])
                 made = (base.astype(jnp.float32) * other).astype(jnp.bfloat16)
-                held[rows, here] = made
+                held[:, here] = made
                 if held is up:
                     acc = acc + made.astype(jnp.float32) * source_ref[:, here]
         return acc
 
-    return lax.fori_loop(0, SIDE, build, jnp.zeros((HALF, 128), jnp.float32))
+    acc = jnp.zeros((HALF, 128), jnp.float32)
+    for chosen, copies in stages:
+        for copy in copies:
+            copy.wait()
+        acc = lax.fori_loop(0, SIDE, functools.partial(build, spins[chosen]), acc)
+    return acc
 
 
 def prepare(index_ref, own_ref, source_ref, up_ref, down_ref, sums_ref):
-    sums_ref[...] = gather_products(index_ref, own_ref, source_ref, up_ref, down_ref, 0)
+    stages = ((slice(0, 2), ()),)
+    sums_ref[...] = gather_products(index_ref, own_ref, source_ref, up_ref, down_ref, stages)
 
 
 def three_rows(row):
@@ -85,10 +91,18 @@
 
 def contract(
     index_ref, up_ref, down_ref, sums_ref, other_ref, source_ref, g4_ref, out_ref,
-    up_other, down_other, left, stage, sems, norm, scale,
+    up_other, down_other, left, stage, sems, raw, load_sems, norm, scale,
 ):
     site = index_ref[2]
-    sums = gather_products(index_ref, other_ref, source_ref, up_other, down_other, 0)
+    spans = (pl.ds(UP_TAIL, PACKET - UP_TAIL), pl.ds(UP, CELLS), pl.ds(DOWN, CELLS))
+    loads = [
+        pltpu.make_async_copy(other_ref.at[:, span], raw.at[:, span], load_sems.at[i])
+        for i, span in enumerate(spans)
+    ]
+    for load in loads:
+        load.start()
+    stages = ((slice(0, 1), loads[:2]), (slice(1, 2), loads[2:]))
+    sums = gather_products(index_ref, raw, source_ref, up_other, down_other, stages)
     first = jnp.concatenate(
         [jnp.sum(part.T, axis=0, keepdims=True) for part in (sums_ref[...], sums)], axis=1
     )
@@ -190,7 +204,7 @@
             jax.ShapeDtypeStruct((W, CELLS), jnp.float32),
             jax.ShapeDtypeStruct((1, W), jnp.float32),
         ),
-        in_specs=[smem, vmem, vmem, vmem, vmem, vmem],
+        in_specs=[smem, vmem, vmem, vmem, pl.BlockSpec(memory_space=pl.ANY), vmem],
         out_specs=(pl.BlockSpec(memory_space=pl.ANY), vmem),
         scratch_shapes=[
             pltpu.VMEM((HALF, CELLS), jnp.bfloat16),
@@ -198,6 +212,8 @@
             pltpu.VMEM((128, HALF), jnp.float32),
             pltpu.VMEM((W, CELLS), jnp.float32),
             pltpu.SemaphoreType.DMA((SIDE,)),
+            pltpu.VMEM((HALF, PACKET), jnp.bfloat16),
+            pltpu.SemaphoreType.DMA((3,)),
         ],
         compiler_params=limit,
     )(index, up, down, sums, other, whole)

time: 70.5 us -> 71.4 us (1.013)
  Pallas kernels: 11.4 us -> 12.3 us
    pallas_call x1, Pallas kernels: 7.79 us -> 8.72 us  [shards(): pl.pallas_call(functools.partial(contract, norm=norm, scale=scale), out_s...]
where the time goes in v5:
time: 71.4 us; the launch traced here: 71.1 us
  blocking collectives  50.2 us (70%)
  Pallas kernels  12.3 us (17%)
  starting transfers between devices  3.92 us (5%)
  between operations  2.02 us (3%)
  other arithmetic  1.62 us (2%)
  local copies, waits for them, and re-layouts  1.02 us (1%)
    all_to_all x1, blocking collectives, shards(): lax.all_to_all(jnp.broadcast_to(rows, (16,) + rows.shape), ('x_hi', 'x_lo...  33.5 us
    all_to_all x1, blocking collectives, shards(): lax.all_to_all(jnp.broadcast_to(packet, (8,) + packet.shape), 'z', 0, 0)  16.7 us
    pallas_call x1, Pallas kernels, shards(): pl.pallas_call(functools.partial(contract, norm=norm, scale=scale), out_s...  8.72 us
    ppermute x1, starting transfers between devices, shards(): other = lax.ppermute(own, 'core', [(0, 1), (1, 0)])  3.92 us
    pallas_call x1, Pallas kernels, shards(): pl.pallas_call(prepare, out_shape=(jax.ShapeDtypeStruct((HALF, CELLS), jn...  3.58 us
  transfers between devices with their start and end apart: 1, of which 0 were waited for; matrix products, arithmetic and copies ran while one was open for 0% of the time, Pallas kernels for 5%

profile of v5, /device:TPU:1, one launch (start us, length us, event | category | flops | bytes accessed | tf_op | source)
XLA Modules:
  0.0 71.1 jit_solution(2821955274272730574)
XLA Ops:
  0.6 0.7 fusion
  1.3 0.8 %pad_maximum_fusion = bf16[2,4288]{1,0:T(2,128)(2,1)S(1)} fusion(bf16[1,4288]{1,0:T(2,128)(2,1)} %bitcast.31, bf16[1,4288]{1,0:T(2,128)(2,1)} %bitcast.32), kind=kLoop, calls=%fused_computation.4 | loop fusion | flops 34304 | bytes 34304 | tf_op jit(solution)/shard_map/concatenate | solution.py:153
  2.1 0.2 reshape.45
  2.2 0.1 fusion.1
  2.3 0.1 reshape.46
  2.4 0.1 squeeze.9
  2.6 0.1 squeeze.8
  2.7 0.1 concatenate.7
  2.8 16.7 %all_to_all.10 = bf16[8,69,128]{2,1,0:T(8,128)(2,1)S(1)} all-to-all(bf16[8,69,128]{2,1,0:T(8,128)(2,1)S(1)} %broadcast_in_dim.10), channel_id=1, replica_groups=mesh['x_hi'=2,'y'=4,'z'=8,'x_lo'=2,'core'=2] {'z'}, dimensions={0} | all-to-all | bytes 282624 | tf_op jit(solution)/shard_map/all_to_all | solution.py:175
  19.6 0.1 broadcast_in_dim.11
  19.7 33.5 %all_to_all.11 = bf16[16,8,8832]{2,1,0:T(8,128)(2,1)S(1)} all-to-all(bf16[16,8,8832]{2,1,0:T(8,128)(2,1)S(1)} %broadcast_in_dim.11), channel_id=1, replica_groups=mesh['x_hi'=2,'y'=4,'z'=8,'x_lo'=2,'core'=2] {'x_hi','x_lo','y'}, dimensions={0} | all-to-all | bytes 4521984 | tf_op jit(solution)/shard_map/all_to_all | solution.py:177
  53.3 3.9 %collective-permute-start = (bf16[128,8832]{1,0:T(8,128)(2,1)S(1)}, bf16[128,8832]{1,0:T(8,128)(2,1)}, u32[]{:S(2)}, u32[]{:S(2)}) collective-permute-start(bf16[128,8832]{1,0:T(8,128)(2,1)S(1)} %bitcast.24), channel_id=1, source_target_pairs={{0,1},{1,0},{2,3},{3,2},{4,5},{5,4},{6,7},{7,6},{8,9},{9,8},{10,11... | collective-permute-start | bytes 6782984 | tf_op jit(solution)/shard_map/ppermute | solution.py:179
  58.5 0.1 pad_add_fusion.index_ref
  58.6 0.1 slice_add_fusion
  58.7 0.1 reshape.51.source_ref
  58.8 3.6 %shard_map.68 = (bf16[128,4096]{1,0:T(8,128)(2,1)S(1)}, bf16[128,4096]{1,0:T(8,128)(2,1)S(1)}, f32[128,128]{1,0:T(8,128)S(1)}) custom-call(s32[3]{0:T(128)S(1)} %pad_add_fusion.index_ref, bf16[128,8832]{1,0:T(8,128)(2,1)S(1)} %bitcast.26, f32[1,4096]{1,0:T(1,128)S(1)} %reshape.51.source_ref), custom_call_target="tpu_custom_call" | custom-call | tf_op jit(solution)/shard_map/pallas_call | solution.py:190
  62.4 0.0 collective-permute-done.other_ref
  62.4 8.7 %shard_map.69 = (f32[64,4096]{1,0:T(8,128)}, f32[1,64]{1,0:T(1,128)}) custom-call(s32[3]{0:T(128)S(1)} %pad_add_fusion.index_ref, bf16[128,4096]{1,0:T(8,128)(2,1)S(1)} %get-tuple-element.7.up_ref, bf16[128,4096]{1,0:T(8,128)(2,1)S(1)} %get-tuple-element.8.down_ref, f32[128,128]{1,0:T(8,128)S(1)} %get-tuple-element.9.sums_ref, ...), custom_call_target="tpu_custom_call" | custom-call | tf_op jit(solution)/shard_map/pallas_call | solution.py:201
  (6 shorter events, 0.1 us)
Async XLA Ops:
  53.3 9.1 %collective-permute-start = (bf16[128,8832]{1,0:T(8,128)(2,1)S(1)}, bf16[128,8832]{1,0:T(8,128)(2,1)}, u32[]{:S(2)}, u32[]{:S(2)}) collective-permute-start(bf16[128,8832]{1,0:T(8,128)(2,1)S(1)} %bitcast.24), channel_id=1, source_target_pairs={{0,1},{1,0},{2,3},{3,2},{4,5},{5,4},{6,7},{7,6},{8,9},{9,8},{10,11... | collective-permute-start | bytes 6782984 | tf_op jit(solution)/shard_map/ppermute | solution.py:179

commit v6 on v3

--- a/solution.py
+++ b/solution.py
@@ -25,7 +25,7 @@
 ROWS = 2 * HALF
 
 
-def gather_products(index_ref, ref, source_ref, up, down, start_row):
+def gather_products(index_ref, ref, source_ref, up, down, start_row, select, make):
     shift_major, shift_minor = index_ref[0] // SIDE, index_ref[0] % SIDE
     offset = index_ref[1]
     rows = pl.ds(start_row, HALF)
@@ -44,8 +44,13 @@
 
     def build(a, acc):
         moved = (a + shift_major) & (SIDE - 1)
-        tail_select = jnp.where(row == wanted + moved * SIDE * (NU - 1), 1.0, 0.0)
-        tail_select = tail_select.astype(jnp.bfloat16)
+        block = pl.ds(pl.multiple_of(a * GROUP, GROUP), GROUP)
+        if make:
+            tail_select = jnp.where(row == wanted + moved * SIDE * (NU - 1), 1.0, 0.0)
+            tail_select = tail_select.astype(jnp.bfloat16)
+            select[:, block] = tail_select
+        else:
+            tail_select = select[:, block]
         for start, tail, held in ((UP, UP_TAIL, up), (DOWN, DOWN_TAIL, down)):
             wrapped = jnp.dot(
                 ref[:, tail : tail + 256], tail_select, preferred_element_type=jnp.float32
@@ -69,16 +74,20 @@
     return lax.fori_loop(0, SIDE, build, jnp.zeros((HALF, 128), jnp.float32))
 
 
-def prepare(index_ref, own_ref, source_ref, up_ref, down_ref, sums_ref):
-    sums_ref[...] = gather_products(index_ref, own_ref, source_ref, up_ref, down_ref, 0)
+def prepare(index_ref, own_ref, source_ref, up_ref, down_ref, sums_ref, select_ref):
+    sums_ref[...] = gather_products(
+        index_ref, own_ref, source_ref, up_ref, down_ref, 0, select_ref, True
+    )
 
 
 def contract(
-    index_ref, up_ref, down_ref, sums_ref, other_ref, source_ref, g4_ref, out_ref,
+    index_ref, up_ref, down_ref, sums_ref, select_ref, other_ref, source_ref, g4_ref, out_ref,
     up_other, down_other, left, norm, scale,
 ):
     site = index_ref[2]
-    sums = gather_products(index_ref, other_ref, source_ref, up_other, down_other, 0)
+    sums = gather_products(
+        index_ref, other_ref, source_ref, up_other, down_other, 0, select_ref, False
+    )
     first = (
         jnp.sum(sums_ref[...], axis=1, keepdims=True),
         jnp.sum(sums, axis=1, keepdims=True),
@@ -159,15 +168,16 @@
     vmem = pl.BlockSpec(memory_space=pltpu.VMEM)
     smem = pl.BlockSpec(memory_space=pltpu.SMEM)
     limit = pltpu.CompilerParams(vmem_limit_bytes=48 * 1024 * 1024)
-    up, down, sums = pl.pallas_call(
+    up, down, sums, select = pl.pallas_call(
         prepare,
         out_shape=(
             jax.ShapeDtypeStruct((HALF, CELLS), jnp.bfloat16),
             jax.ShapeDtypeStruct((HALF, CELLS), jnp.bfloat16),
             jax.ShapeDtypeStruct((HALF, 128), jnp.float32),
+            jax.ShapeDtypeStruct((256, CELLS), jnp.bfloat16),
         ),
         in_specs=[smem, vmem, vmem],
-        out_specs=(vmem, vmem, vmem),
+        out_specs=(vmem, vmem, vmem, vmem),
         compiler_params=limit,
     )(index, own, whole)
     g4, answer = pl.pallas_call(
@@ -176,7 +186,7 @@
             jax.ShapeDtypeStruct((W, CELLS), jnp.float32),
             jax.ShapeDtypeStruct((1, W), jnp.float32),
         ),
-        in_specs=[smem, vmem, vmem, vmem, vmem, vmem],
+        in_specs=[smem, vmem, vmem, vmem, vmem, vmem, vmem],
         out_specs=(vmem, vmem),
         scratch_shapes=[
             pltpu.VMEM((HALF, CELLS), jnp.bfloat16),
@@ -184,7 +194,7 @@
             pltpu.VMEM((128, HALF), jnp.float32),
         ],
         compiler_params=limit,
-    )(index, up, down, sums, other, whole)
+    )(index, up, down, sums, select, other, whole)
     return g4.reshape(1, W, CELLS), answer
 
 

time: 70.4 us -> 71.4 us (1.014)
  Pallas kernels: 11.3 us -> 12.3 us
    pallas_call x1, Pallas kernels: 3.59 us -> 4.92 us  [shards(): pl.pallas_call(prepare, out_shape=(jax.ShapeDtypeStruct((HALF, CELLS), jn...]
  transfers between devices with their start and end apart: 1 -> 1, of which waited for: 0 -> 0; matrix products, arithmetic and copies ran while one was open for 0% -> 0% of each run, Pallas kernels for 5% -> 7%
where the time goes in v6:
time: 71.4 us; the launch traced here: 71.1 us
  blocking collectives  50.2 us (70%)
  Pallas kernels  12.3 us (17%)
  starting transfers between devices  3.92 us (5%)
  between operations  2.03 us (3%)
  other arithmetic  1.62 us (2%)
  local copies, waits for them, and re-layouts  1.02 us (1%)
    all_to_all x1, blocking collectives, shards(): lax.all_to_all(jnp.broadcast_to(rows, (16,) + rows.shape), ('x_hi', 'x_lo...  33.5 us
    all_to_all x1, blocking collectives, shards(): lax.all_to_all(jnp.broadcast_to(packet, (8,) + packet.shape), 'z', 0, 0)  16.7 us
    pallas_call x1, Pallas kernels, shards(): pl.pallas_call(functools.partial(contract, norm=norm, scale=scale), out_s...  7.35 us
    pallas_call x1, Pallas kernels, shards(): pl.pallas_call(prepare, out_shape=(jax.ShapeDtypeStruct((HALF, CELLS), jn...  4.92 us
    ppermute x1, starting transfers between devices, shards(): other = lax.ppermute(own, 'core', [(0, 1), (1, 0)])  3.92 us
  transfers between devices with their start and end apart: 1, of which 0 were waited for; matrix products, arithmetic and copies ran while one was open for 0% of the time, Pallas kernels for 7%

profile of v6, /device:TPU:1, one launch (start us, length us, event | category | flops | bytes accessed | tf_op | source)
XLA Modules:
  0.0 71.1 jit_solution(12051838898272029865)
XLA Ops:
  0.6 0.7 fusion
  1.3 0.8 %pad_maximum_fusion = bf16[2,4288]{1,0:T(2,128)(2,1)S(1)} fusion(bf16[1,4288]{1,0:T(2,128)(2,1)} %bitcast.31, bf16[1,4288]{1,0:T(2,128)(2,1)} %bitcast.32), kind=kLoop, calls=%fused_computation.4 | loop fusion | flops 34304 | bytes 34304 | tf_op jit(solution)/shard_map/concatenate | solution.py:134
  2.1 0.2 reshape.45
  2.2 0.1 fusion.1
  2.3 0.1 reshape.46
  2.4 0.1 squeeze.9
  2.6 0.1 squeeze.8
  2.7 0.1 concatenate.7
  2.8 16.7 %all_to_all.10 = bf16[8,69,128]{2,1,0:T(8,128)(2,1)S(1)} all-to-all(bf16[8,69,128]{2,1,0:T(8,128)(2,1)S(1)} %broadcast_in_dim.10), channel_id=1, replica_groups=mesh['x_hi'=2,'y'=4,'z'=8,'x_lo'=2,'core'=2] {'z'}, dimensions={0} | all-to-all | bytes 282624 | tf_op jit(solution)/shard_map/all_to_all | solution.py:156
  19.6 0.1 broadcast_in_dim.11
  19.7 33.5 %all_to_all.11 = bf16[16,8,8832]{2,1,0:T(8,128)(2,1)S(1)} all-to-all(bf16[16,8,8832]{2,1,0:T(8,128)(2,1)S(1)} %broadcast_in_dim.11), channel_id=1, replica_groups=mesh['x_hi'=2,'y'=4,'z'=8,'x_lo'=2,'core'=2] {'x_hi','x_lo','y'}, dimensions={0} | all-to-all | bytes 4521984 | tf_op jit(solution)/shard_map/all_to_all | solution.py:158
  53.3 0.0 copy-start
  53.3 3.9 %collective-permute-start = (bf16[128,8832]{1,0:T(8,128)(2,1)S(1)}, bf16[128,8832]{1,0:T(8,128)(2,1)}, u32[]{:S(2)}, u32[]{:S(2)}) collective-permute-start(bf16[128,8832]{1,0:T(8,128)(2,1)S(1)} %bitcast.24), channel_id=1, source_target_pairs={{0,1},{1,0},{2,3},{3,2},{4,5},{5,4},{6,7},{7,6},{8,9},{9,8},{10,11... | collective-permute-start | bytes 6782984 | tf_op jit(solution)/shard_map/ppermute | solution.py:160
  58.5 0.1 pad_add_fusion.index_ref
  58.6 0.1 slice_add_fusion
  58.7 0.1 reshape.51.source_ref
  58.8 0.0 copy-done
  58.8 4.9 %shard_map.68 = (bf16[128,4096]{1,0:T(8,128)(2,1)S(1)}, bf16[128,4096]{1,0:T(8,128)(2,1)S(1)}, f32[128,128]{1,0:T(8,128)S(1)}, bf16[256,4096]{1,0:T(8,128)(2,1)S(1)}) custom-call(s32[3]{0:T(128)S(1)} %pad_add_fusion.index_ref, bf16[128,8832]{1,0:T(8,128)(2,1)} %bitcast.26, f32[1,4096]{1,0:T(1,128)S(1)} %reshape.51.source_ref), custom_call_target="tpu_custom_call" | custom-call | tf_op jit(solution)/shard_map/pallas_call | solution.py:171
  63.7 0.0 collective-permute-done.other_ref
  63.8 7.3 %shard_map.69 = (f32[64,4096]{1,0:T(8,128)}, f32[1,64]{1,0:T(1,128)}) custom-call(s32[3]{0:T(128)S(1)} %pad_add_fusion.index_ref, bf16[128,4096]{1,0:T(8,128)(2,1)S(1)} %get-tuple-element.8.up_ref, bf16[128,4096]{1,0:T(8,128)(2,1)S(1)} %get-tuple-element.9.down_ref, f32[128,128]{1,0:T(8,128)S(1)} %get-tuple-element.10.sums_ref, ...), custom_call_target="tpu_custom_call" | custom-call | tf_op jit(solution)/shard_map/pallas_call | solution.py:183
  (6 shorter events, 0.1 us)
Async XLA Ops:
  53.3 5.6 %copy-start = (bf16[16,8,8832]{2,1,0:T(8,128)(2,1)}, bf16[16,8,8832]{2,1,0:T(8,128)(2,1)S(1)}, u32[]{:S(2)}) copy-start(bf16[16,8,8832]{2,1,0:T(8,128)(2,1)S(1)} %all_to_all.11) | copy-start | bytes 6782980
  53.3 10.5 %collective-permute-start = (bf16[128,8832]{1,0:T(8,128)(2,1)S(1)}, bf16[128,8832]{1,0:T(8,128)(2,1)}, u32[]{:S(2)}, u32[]{:S(2)}) collective-permute-start(bf16[128,8832]{1,0:T(8,128)(2,1)S(1)} %bitcast.24), channel_id=1, source_target_pairs={{0,1},{1,0},{2,3},{3,2},{4,5},{5,4},{6,7},{7,6},{8,9},{9,8},{10,11... | collective-permute-start | bytes 6782984 | tf_op jit(solution)/shard_map/ppermute | solution.py:160
